TPU v7x, 128 devices: a whole 4x4x4 slice. The times are simulated.
128 devices in a mesh: group: 8 (over y, core), within: 16 (over z, x).
Axes of the slice: x: 4, y: 4, z: 4, core: 2. Of those that a mesh axis runs over, the one named last changes fastest.
Arguments:
- tokens: bfloat16 [16384, 2048], P(('group', 'within')), may hold values from -6 to 6
- languages: int32 [16384], P(('group', 'within')), may hold values from 0 to 99, as said below
- lang_group: int32 [100], replicated, may hold values from 0 to 7, as said below
- group_gain: float32 [8, 2048], replicated, may hold values from 0.25 to 1.75
- group_w1: bfloat16 [8, 2048, 8192], P('group', None, 'within'), may hold values from -0.125 to 0.125
- group_b1: float32 [8, 8192], P('group', 'within'), may hold values from -3 to 3
- group_w2: bfloat16 [8, 8192, 2048], P('group', 'within'), may hold values from -0.0625 to 0.0625
- group_b2: float32 [8, 2048], replicated, may hold values from -3 to 3
- shared_gain: float32 [2048], replicated, may hold values from 0.25 to 1.75
- shared_w1: bfloat16 [2048, 8192], P(None, 'group'), may hold values from -0.125 to 0.125
- shared_b1: float32 [8192], P('group'), may hold values from -3 to 3
- shared_w2: bfloat16 [8192, 2048], P('group'), may hold values from -0.0625 to 0.0625
- shared_b2: float32 [2048], replicated, may hold values from -3 to 3
Outputs:
- encoded: bfloat16 [16384, 2048], P(('group', 'within'))
Inputs may be any that keep to these rules, and one draw needn't show every extreme that they name: `lang_group`: every language lies in one group and every group holds at least one language. Among the 128 tokens of one device (an aligned block), at most 24 have languages of one group, and in every block some group has exactly 24.
All inputs are finite; a program needn't handle non-finite values.
Results may differ from a plain program's by a relative error of at most 0.017.
Values may be sent and summed in bfloat16 or wider, within the bound.
No kernel may reach another device: no remote copies, remote signals or barrier semaphores. Data moves between devices by JAX's collectives and lax.ppermute only.
A program may use at most 128 MiB of HBM per device.

v0:
```python
import jax
import jax.numpy as jnp
from jax import lax
from jax.sharding import PartitionSpec as P


def layer_norm(values, gains):
    centre = jnp.mean(values, axis=-1, keepdims=True)
    centred = values - centre
    spread = jnp.mean(centred * centred, axis=-1, keepdims=True)
    return centred * lax.rsqrt(spread + 1e-05) * gains


def on_device(
    tokens,
    languages,
    lang_group,
    group_gain,
    group_w1,
    group_b1,
    group_w2,
    group_b2,
    shared_gain,
    shared_w1,
    shared_b1,
    shared_w2,
    shared_b2,
):
    tok_dev = tokens.shape[0]
    width_model = tokens.shape[1]
    num_groups = group_gain.shape[0]
    num_langs = lang_group.shape[0]
    capacity = 3 * tok_dev // (2 * lax.axis_size("group"))
    residual_in = tokens.astype(jnp.float32)
    lang_hit = (languages[:, None] == jnp.arange(num_langs, dtype=jnp.int32)[None, :]).astype(
        jnp.int32
    )
    group_of = jnp.sum(lang_hit * lang_group[None, :], axis=1)
    onehot = (group_of[:, None] == jnp.arange(num_groups, dtype=jnp.int32)[None, :]).astype(
        jnp.int32
    )
    earlier = jnp.cumsum(onehot, axis=0) - onehot
    slot_index = jnp.sum(earlier * onehot, axis=1)
    position = group_of * capacity + slot_index
    dispatch_map = (
        position[None, :] == jnp.arange(num_groups * capacity, dtype=jnp.int32)[:, None]
    ).astype(jnp.bfloat16)
    onehot_float = onehot.astype(jnp.float32)
    row_gains = jnp.dot(onehot_float, group_gain, precision=lax.Precision.HIGHEST)
    normed = layer_norm(residual_in, row_gains).astype(jnp.bfloat16)
    outgoing = jnp.dot(dispatch_map, normed, preferred_element_type=jnp.float32).astype(
        jnp.bfloat16
    )
    outgoing = outgoing.reshape(num_groups, capacity, width_model)
    arrived = lax.all_to_all(outgoing, "group", split_axis=0, concat_axis=0, tiled=True)
    group_rows = arrived.reshape(num_groups * capacity, width_model)
    first_proj = group_w1[0]
    first_bias = group_b1[0]
    second_proj = group_w2[0]
    hidden = jax.nn.relu(
        jnp.dot(
            lax.all_gather(group_rows, "within", axis=0, tiled=True),
            first_proj,
            preferred_element_type=jnp.float32,
        )
        + first_bias
    ).astype(jnp.bfloat16)
    selected = hidden
    summed = lax.psum_scatter(
        jnp.dot(selected, second_proj, preferred_element_type=jnp.float32).astype(jnp.bfloat16),
        "within",
        scatter_dimension=0,
        tiled=True,
    )
    returned = lax.all_to_all(
        summed.reshape(num_groups, capacity, width_model),
        "group",
        split_axis=0,
        concat_axis=0,
        tiled=True,
    )
    returned = returned.reshape(num_groups * capacity, width_model)
    group_out = lax.dot_general(
        dispatch_map, returned, (((0,), (0,)), ((), ())), preferred_element_type=jnp.float32
    )
    group_bias = jnp.dot(onehot_float, group_b2, precision=lax.Precision.HIGHEST)
    middle = residual_in + group_out + group_bias
    shared_in = layer_norm(middle, shared_gain).astype(jnp.bfloat16)
    shared_hidden = jax.nn.relu(
        jnp.dot(
            lax.all_gather(shared_in, "group", axis=0, tiled=True),
            shared_w1,
            preferred_element_type=jnp.float32,
        )
        + shared_b1
    ).astype(jnp.bfloat16)
    selected = shared_hidden
    shared_out = lax.psum_scatter(
        jnp.dot(selected, shared_w2, preferred_element_type=jnp.float32).astype(jnp.bfloat16),
        "group",
        scatter_dimension=0,
        tiled=True,
    ).astype(jnp.float32)
    return (middle + shared_out + shared_b2).astype(jnp.bfloat16)


def solution(mesh):
    placed = (
        P(("group", "within"), None),
        P(("group", "within")),
        P(),
        P(),
        P("group", None, "within"),
        P("group", "within"),
        P("group", "within", None),
        P(),
        P(),
        P(None, "group"),
        P("group"),
        P("group", None),
        P(),
    )
    return jax.shard_map(
        on_device,
        mesh=mesh,
        in_specs=placed,
        out_specs=P(("group", "within"), None),
        check_vma=False,
    )
```

profile of v0, /device:TPU:0, one launch (start us, length us, event | category | flops | bytes accessed | tf_op | source)
XLA Modules:
  0.0 346.0 jit_solution(16796450870467543149)
XLA Ops:
  6.5 1.3 convert_reduce_fusion
  7.9 1.3 fusion.10
  9.2 0.8 select_reduce_fusion
  10.0 0.1 fusion.17
  10.1 0.2 reduce_window_sum.11
  10.3 0.2 fusion.16
  10.5 2.2 fusion
  12.6 0.4 convolution_convert_fusion.2
  13.0 17.7 %all_to_all.10 = bf16[8,24,2048]{2,1,0:T(8,128)(2,1)} all-to-all(bf16[8,24,2048]{2,1,0:T(8,128)(2,1)S(1)} %bitcast.22), channel_id=1, replica_groups=mesh['group'=8,'within'=16] {'group'}, dimensions={0} | all-to-all | bytes 1572864 | tf_op jit(solution)/shard_map/all_to_all | solution.py:55
  30.7 0.0 reduce-scatter.3.cloned.1.call-start
  30.8 90.6 %all-gather.3.cloned.1.call-done = bf16[3072,2048]{1,0:T(8,128)(2,1)} async-done(((bf16[192,2048]{1,0:T(8,128)(2,1)}), bf16[3072,2048]{1,0:T(8,128)(2,1)}) %all-gather.3.cloned.1.call-update) | async-done | bytes 12582928 | tf_op jit(solution)/shard_map/all_gather | solution.py:62
  121.4 19.5 %convolution_convert_fusion = bf16[3072,2048]{1,0:T(8,128)(2,1)} fusion(bf16[1,512,2048]{2,1,0:T(8,128)(2,1)S(1)} %copy-done, bf16[3072,2048]{1,0:T(8,128)(2,1)} %all-gather.3.cloned.1.call-done, f32[512]{0:T(512)S(1)} %bitcast.24, bf16[1,2048,512]{2,1,0:T(8,128)(2,1)} %param.17), kind=kOutput, calls=%fused_computation | convolution fusion | flops 12895911936 | bytes 29362176 | tf_op jit(solution)/shard_map/dot_general | solution.py:70
  140.9 0.0 all-gather.5.cloned.1.call-start
  140.9 94.3 %reduce-scatter.3.cloned.1.call-done = bf16[192,2048]{1,0:T(8,128)(2,1)} async-done(((bf16[3072,2048]{1,0:T(8,128)(2,1)}), bf16[192,2048]{1,0:T(8,128)(2,1)}) %reduce-scatter.3.cloned.1.call-update) | async-done | bytes 786448 | tf_op jit(solution)/shard_map/reduce_scatter | solution.py:69
  235.2 17.5 %all_to_all.11 = bf16[8,24,2048]{2,1,0:T(8,128)(2,1)S(1)} all-to-all(bf16[8,24,2048]{2,1,0:T(8,128)(2,1)} %bitcast.23), channel_id=1, replica_groups=mesh['group'=8,'within'=16] {'group'}, dimensions={0} | all-to-all | bytes 1572864 | tf_op jit(solution)/shard_map/all_to_all | solution.py:75
  252.7 0.4 convolution_add_fusion.1
  253.1 1.1 fusion.24
  254.3 0.3 multiply_reduce_fusion
  254.5 1.0 multiply_convert_fusion
  255.6 0.2 reduce-scatter.5.cloned.1.call-start
  255.8 29.2 %all-gather.5.cloned.1.call-done = bf16[1024,2048]{1,0:T(8,128)(2,1)} async-done(((bf16[128,2048]{1,0:T(8,128)(2,1)}), bf16[1024,2048]{1,0:T(8,128)(2,1)}) %all-gather.5.cloned.1.call-update) | async-done | bytes 4194320 | tf_op jit(solution)/shard_map/all_gather | solution.py:91
  285.0 14.3 %convolution_convert_fusion.1 = bf16[1024,2048]{1,0:T(8,128)(2,1)} fusion(bf16[1024,2048]{1,0:T(8,128)(2,1)} %param.24, f32[1024]{0:T(1024)S(1)} %copy-done.5, bf16[1024,2048]{1,0:T(8,128)(2,1)} %all-gather.5.cloned.1.call-done, bf16[2048,1024]{1,0:T(8,128)(2,1)} %param.22), kind=kOutput, calls=%fused_computation.3 | convolution fusion | flops 8595177472 | bytes 16781312 | tf_op jit(solution)/shard_map/dot_general | solution.py:99
  299.4 38.1 %reduce-scatter.5.cloned.1.call-done = bf16[128,2048]{1,0:T(8,128)(2,1)} async-done(((bf16[1024,2048]{1,0:T(8,128)(2,1)}), bf16[128,2048]{1,0:T(8,128)(2,1)}) %reduce-scatter.5.cloned.1.call-update) | async-done | bytes 524304 | tf_op jit(solution)/shard_map/reduce_scatter | solution.py:98
  337.5 2.0 add_convert_fusion
  (24 shorter events, 0.1 us)
Async XLA Ops:
  6.5 114.8 %copy-start = (bf16[1,512,2048]{2,1,0:T(8,128)(2,1)S(1)}, bf16[1,512,2048]{2,1,0:T(8,128)(2,1)}, u32[]{:S(2)}) copy-start(bf16[1,512,2048]{2,1,0:T(8,128)(2,1)} %param.19) | copy-start | bytes 6291460
  6.5 114.8 %copy-start.6 = (f32[1,512]{1,0:T(1,128)S(1)}, f32[1,512]{1,0:T(1,128)}, u32[]{:S(2)}) copy-start(f32[1,512]{1,0:T(1,128)} %param.18) | copy-start | bytes 6148
  6.5 114.8 %all-gather.3.cloned.1.call-start = ((), (), s32[]{:S(2)}) async-start(), calls=%async_computation.4 | async-start | bytes 13369344 | tf_op jit(solution)/shard_map/all_gather | solution.py:62
  30.7 204.5 %reduce-scatter.3.cloned.1.call-start = ((), (), s32[]{:S(2)}) async-start(), calls=%async_computation.5 | async-start | bytes 13369344 | tf_op jit(solution)/shard_map/reduce_scatter | solution.py:69
  140.8 111.9 %copy-start.1 = (bf16[128,2048]{1,0:T(8,128)(2,1)S(1)}, bf16[128,2048]{1,0:T(8,128)(2,1)}, u32[]{:S(2)}) copy-start(bf16[128,2048]{1,0:T(8,128)(2,1)} %param.13) | copy-start | bytes 1572868
  140.8 112.3 %copy-start.2 = (f32[8,2048]{1,0:T(8,128)S(1)}, f32[8,2048]{1,0:T(8,128)}, u32[]{:S(2)}) copy-start(f32[8,2048]{1,0:T(8,128)} %param.20) | copy-start | bytes 196612
  140.9 113.7 %copy-start.3 = (f32[2048]{0:T(1024)S(1)}, f32[2048]{0:T(1024)}, u32[]{:S(2)}) copy-start(f32[2048]{0:T(1024)} %param.21) | copy-start | bytes 24580
  140.9 144.1 %all-gather.5.cloned.1.call-start = ((), (), s32[]{:S(2)}) async-start(), calls=%async_computation.6 | async-start | bytes 4718592 | tf_op jit(solution)/shard_map/all_gather | solution.py:91
  252.7 32.3 %copy-start.5 = (f32[1024]{0:T(1024)S(1)}, f32[1024]{0:T(1024)}, u32[]{:S(2)}) copy-start(f32[1024]{0:T(1024)} %param.23) | copy-start | bytes 12292
  255.6 81.9 %reduce-scatter.5.cloned.1.call-start = ((), (), s32[]{:S(2)}) async-start(), calls=%async_computation.7 | async-start | bytes 4718592 | tf_op jit(solution)/shard_map/reduce_scatter | solution.py:98
  299.3 38.1 %copy-start.4 = (f32[2048]{0:T(1024)S(1)}, f32[2048]{0:T(1024)}, u32[]{:S(2)}) copy-start(f32[2048]{0:T(1024)} %param.25) | copy-start | bytes 24580
Sparse Core Ops, SparseCore 0:
  30.8 90.4 all-gather.2
  141.0 94.1 reduce-scatter.2
  255.7 29.2 all-gather.4
  299.5 37.9 reduce-scatter.4
where the time goes:
time: 346 us
  waiting for transfers between devices  252 us (73%)
  matrix products  37.8 us (11%)
  blocking collectives  35.2 us (10%)
  between operations  13.2 us (4%)
  other arithmetic  7.17 us (2%)
    reduce_scatter x1, waiting for transfers between devices, on_device(): lax.psum_scatter(jnp.dot(selected, second_proj, preferred_element_type=jn...  94.3 us
    all_gather x1, waiting for transfers between devices, on_device(): lax.all_gather(group_rows, 'within', axis=0, tiled=True)  90.6 us
    reduce_scatter x1, waiting for transfers between devices, on_device(): lax.psum_scatter(jnp.dot(selected, shared_w2, preferred_element_type=jnp....  38.1 us
    all_gather x1, waiting for transfers between devices, on_device(): lax.all_gather(shared_in, 'group', axis=0, tiled=True)  29.2 us
    dot_general x1, matrix products, on_device(): jnp.dot(selected, second_proj, preferred_element_type=jnp.float32)  19.5 us
    all_to_all x1, blocking collectives, on_device(): lax.all_to_all(outgoing, 'group', split_axis=0, concat_axis=0, tiled=True)  17.7 us
    all_to_all x1, blocking collectives, on_device(): lax.all_to_all(summed.reshape(num_groups, capacity, width_model), 'group'...  17.5 us
    dot_general x1, matrix products, on_device(): jnp.dot(selected, shared_w2, preferred_element_type=jnp.float32)  14.3 us
  transfers between devices with their start and end apart: 4, of which 4 were waited for; matrix products, arithmetic and copies ran while one was open for 0% of the time, Pallas kernels for 0%

commit v1 on v0

--- a/solution.py
+++ b/solution.py
@@ -2,6 +2,27 @@
 import jax.numpy as jnp
 from jax import lax
 from jax.sharding import PartitionSpec as P
+
+
+def ring_gather(x, axis, dim):
+    count, index, rows = (lax.axis_size(axis), lax.axis_index(axis), x.shape[dim])
+    forward = [(i, (i + 1) % count) for i in range(count)]
+    backward = [(i, (i - 1) % count) for i in range(count)]
+    out = jnp.zeros((*x.shape[:dim], count * rows, *x.shape[dim + 1 :]), x.dtype)
+    out = lax.dynamic_update_slice_in_dim(out, x, index * rows, axis=dim)
+    from_left = from_right = x
+    half = count // 2
+    for step in range(1, half + 1):
+        from_left = lax.ppermute(from_left, axis, forward)
+        out = lax.dynamic_update_slice_in_dim(
+            out, from_left, (index - step) % count * rows, axis=dim
+        )
+        if step < count - half:
+            from_right = lax.ppermute(from_right, axis, backward)
+            out = lax.dynamic_update_slice_in_dim(
+                out, from_right, (index + step) % count * rows, axis=dim
+            )
+    return out
 
 
 def layer_norm(values, gains):
@@ -87,11 +108,7 @@
     middle = residual_in + group_out + group_bias
     shared_in = layer_norm(middle, shared_gain).astype(jnp.bfloat16)
     shared_hidden = jax.nn.relu(
-        jnp.dot(
-            lax.all_gather(shared_in, "group", axis=0, tiled=True),
-            shared_w1,
-            preferred_element_type=jnp.float32,
-        )
+        jnp.dot(ring_gather(shared_in, "group", 0), shared_w1, preferred_element_type=jnp.float32)
         + shared_b1
     ).astype(jnp.bfloat16)
     selected = shared_hidden

time: 346 us -> 357 us (1.032)
  blocking collectives: 35.2 us -> 17.7 us
  starting transfers between devices: 0.31 us -> 13.4 us
  local copies, waits for them, and re-layouts: 0.03 us -> 12.6 us
    all_gather x1 -> x0, waiting for transfers between devices: 29.2 us -> none  [on_device(): lax.all_gather(shared_in, 'group', axis=0, tiled=True)]
    ppermute x0 -> x7, waiting for transfers between devices: none -> 21.8 us  [the longest x4 20.9 us: ring_gather(): from_left = lax.ppermute(from_left, axis, forward)]
    all_to_all x1 -> x0, blocking collectives: 17.5 us -> none  [on_device(): lax.all_to_all(summed.reshape(num_groups, capacity, width_model), 'group'...]
    all_to_all x0 -> x1, waiting for transfers between devices: none -> 12.9 us  [on_device(): lax.all_to_all(summed.reshape(num_groups, capacity, width_model), 'group'...]
    dynamic_update_slice x0 -> x7, local copies, waits for them, and re-layouts: none -> 10.1 us  [the longest x4 5.47 us: ring_gather(): lax.dynamic_update_slice_in_dim(out, from_left, (index - step) % count *...]
    ppermute x0 -> x7, starting transfers between devices: none -> 8.81 us  [the longest x3 8.8 us: ring_gather(): from_right = lax.ppermute(from_right, axis, backward)]
    all_to_all x0 -> x1, starting transfers between devices: none -> 4.29 us  [on_device(): lax.all_to_all(summed.reshape(num_groups, capacity, width_model), 'group'...]
  transfers between devices with their start and end apart: 4 -> 11, of which waited for: 4 -> 9; matrix products, arithmetic and copies ran while one was open for 0% -> 3% of each run, Pallas kernels for 0% -> 0%
where the time goes in v1:
time: 357 us; the launch traced here: 356 us
  waiting for transfers between devices  255 us (71%)
  matrix products  37.8 us (11%)
  blocking collectives  17.7 us (5%)
  starting transfers between devices  13.4 us (4%)
  between operations  13.2 us (4%)
  local copies, waits for them, and re-layouts  12.6 us (4%)
  other arithmetic  7.15 us (2%)
    reduce_scatter x1, waiting for transfers between devices, on_device(): lax.psum_scatter(jnp.dot(selected, second_proj, preferred_element_type=jn...  94.4 us
    all_gather x1, waiting for transfers between devices, on_device(): lax.all_gather(group_rows, 'within', axis=0, tiled=True)  90.6 us
    reduce_scatter x1, waiting for transfers between devices, on_device(): lax.psum_scatter(jnp.dot(selected, shared_w2, preferred_element_type=jnp....  34.7 us
    ppermute x4, waiting for transfers between devices, ring_gather(): from_left = lax.ppermute(from_left, axis, forward)  20.9 us
    dot_general x1, matrix products, on_device(): jnp.dot(selected, second_proj, preferred_element_type=jnp.float32)  19.4 us
    all_to_all x1, blocking collectives, on_device(): lax.all_to_all(outgoing, 'group', split_axis=0, concat_axis=0, tiled=True)  17.7 us
    dot_general x1, matrix products, on_device(): jnp.dot(selected, shared_w2, preferred_element_type=jnp.float32)  14.4 us
    all_to_all x1, waiting for transfers between devices, on_device(): lax.all_to_all(summed.reshape(num_groups, capacity, width_model), 'group'...  12.9 us
  transfers between devices with their start and end apart: 11, of which 9 were waited for; matrix products, arithmetic and copies ran while one was open for 3% of the time, Pallas kernels for 0%

profile of v1, /device:TPU:0, one launch (start us, length us, event | category | flops | bytes accessed | tf_op | source)
XLA Modules:
  0.0 356.4 jit_solution(5221112802749200692)
XLA Ops:
  6.5 1.3 convert_reduce_fusion
  7.9 1.3 fusion.10
  10.5 2.2 fusion
  13.0 17.7 %all_to_all.10 = bf16[8,24,2048]{2,1,0:T(8,128)(2,1)} all-to-all(bf16[8,24,2048]{2,1,0:T(8,128)(2,1)S(1)} %bitcast.22), channel_id=1, replica_groups=mesh['group'=8,'within'=16] {'group'}, dimensions={0} | all-to-all | bytes 1572864 | tf_op jit(solution)/shard_map/all_to_all | solution.py:76
  30.8 90.6 %all-gather.2.cloned.1.call-done = bf16[3072,2048]{1,0:T(8,128)(2,1)} async-done(((bf16[192,2048]{1,0:T(8,128)(2,1)}), bf16[3072,2048]{1,0:T(8,128)(2,1)}) %all-gather.2.cloned.1.call-update) | async-done | bytes 12582928 | tf_op jit(solution)/shard_map/all_gather | solution.py:83
  121.4 19.4 %convolution_convert_fusion = bf16[3072,2048]{1,0:T(8,128)(2,1)} fusion(bf16[1,512,2048]{2,1,0:T(8,128)(2,1)S(1)} %copy-done, bf16[3072,2048]{1,0:T(8,128)(2,1)} %all-gather.2.cloned.1.call-done, f32[512]{0:T(512)S(1)} %bitcast.24, bf16[1,2048,512]{2,1,0:T(8,128)(2,1)} %param.17), kind=kOutput, calls=%fused_computation | convolution fusion | flops 12895911936 | bytes 29362176 | tf_op jit(solution)/shard_map/dot_general | solution.py:91
  140.9 94.4 %reduce-scatter.3.cloned.1.call-done = bf16[192,2048]{1,0:T(8,128)(2,1)} async-done(((bf16[3072,2048]{1,0:T(8,128)(2,1)}), bf16[192,2048]{1,0:T(8,128)(2,1)}) %reduce-scatter.3.cloned.1.call-update) | async-done | bytes 786448 | tf_op jit(solution)/shard_map/reduce_scatter | solution.py:90
  235.3 4.3 %all-to-all-start.1 = ((bf16[8,24,2048]{2,1,0:T(8,128)(2,1)}), bf16[8,24,2048]{2,1,0:T(8,128)(2,1)S(1)}, u32[]{:S(2)}, u32[]{:S(2)}) async-start(bf16[8,24,2048]{2,1,0:T(8,128)(2,1)} %bitcast.23), calls=%async_computation.2 | async-start | bytes 1572864 | tf_op jit(solution)/shard_map/all_to_all | solution.py:96
  239.8 12.9 %all-to-all-done.1 = bf16[8,24,2048]{2,1,0:T(8,128)(2,1)S(1)} async-done(((bf16[8,24,2048]{2,1,0:T(8,128)(2,1)}), bf16[8,24,2048]{2,1,0:T(8,128)(2,1)S(1)}, u32[]{:S(2)}, u32[]{:S(2)}) %all-to-all-start.1) | async-done | bytes 786464 | tf_op jit(solution)/shard_map/all_to_all | solution.py:96
  254.6 2.5 broadcast_in_dim.2
  258.1 3.0 collective-permute-start.1
  261.0 7.0 %collective-permute-done = bf16[128,2048]{1,0:T(8,128)(2,1)} collective-permute-done((bf16[128,2048]{1,0:T(8,128)(2,1)S(1)}, bf16[128,2048]{1,0:T(8,128)(2,1)}, u32[]{:S(2)}, u32[]{:S(2)}) %collective-permute-start) | collective-permute-done | bytes 524320 | tf_op jit(solution)/shard_map/ppermute | solution.py:16
  268.0 3.0 collective-permute-start.3
  271.0 7.2 %collective-permute-done.2 = bf16[128,2048]{1,0:T(8,128)(2,1)} collective-permute-done((bf16[128,2048]{1,0:T(8,128)(2,1)}, bf16[128,2048]{1,0:T(8,128)(2,1)}, u32[]{:S(2)}, u32[]{:S(2)}) %collective-permute-start.2) | collective-permute-done | bytes 524320 | tf_op jit(solution)/shard_map/ppermute | solution.py:16
  278.1 1.9 constant_dynamic-update-slice_fusion.5
  280.0 1.9 constant_dynamic-update-slice_fusion.4
  281.9 2.9 collective-permute-start.5
  284.8 1.9 constant_dynamic-update-slice_fusion.3
  286.7 1.4 collective-permute-done.4
  288.2 1.9 constant_dynamic-update-slice_fusion.2
  292.7 5.3 %collective-permute-done.6 = bf16[128,2048]{1,0:T(8,128)(2,1)S(1)} collective-permute-done((bf16[128,2048]{1,0:T(8,128)(2,1)S(1)}, bf16[128,2048]{1,0:T(8,128)(2,1)S(1)}, u32[]{:S(2)}, u32[]{:S(2)}) %collective-permute-start.6) | collective-permute-done | bytes 524320 | tf_op jit(solution)/shard_map/ppermute | solution.py:16
  298.8 14.4 %convolution_convert_fusion.1 = bf16[1024,2048]{1,0:T(8,128)(2,1)} fusion(bf16[1024,2048]{1,0:T(8,128)(2,1)} %param.24, f32[1024]{0:T(1024)S(1)} %copy-done.5, bf16[1024,2048]{1,0:T(8,128)(2,1)} %constant_dynamic-update-slice_fusion.7, bf16[2048,1024]{1,0:T(8,128)(2,1)} %param.22), kind=kOutput, calls=%fused_computation.3 | convolution fusion | flops 8595177472 | bytes 16781312 | tf_op jit(solution)/shard_map/dot_general | solution.py:116
  313.2 34.7 %reduce-scatter.5.cloned.1.call-done = bf16[128,2048]{1,0:T(8,128)(2,1)} async-done(((bf16[1024,2048]{1,0:T(8,128)(2,1)}), bf16[128,2048]{1,0:T(8,128)(2,1)}) %reduce-scatter.5.cloned.1.call-update) | async-done | bytes 524304 | tf_op jit(solution)/shard_map/reduce_scatter | solution.py:115
  347.9 2.0 add_convert_fusion
  (44 shorter events, 8.2 us)
Async XLA Ops:
  6.5 114.8 %copy-start = (bf16[1,512,2048]{2,1,0:T(8,128)(2,1)S(1)}, bf16[1,512,2048]{2,1,0:T(8,128)(2,1)}, u32[]{:S(2)}) copy-start(bf16[1,512,2048]{2,1,0:T(8,128)(2,1)} %param.19) | copy-start | bytes 6291460
  6.5 114.8 %copy-start.6 = (f32[1,512]{1,0:T(1,128)S(1)}, f32[1,512]{1,0:T(1,128)}, u32[]{:S(2)}) copy-start(f32[1,512]{1,0:T(1,128)} %param.18) | copy-start | bytes 6148
  6.5 114.8 %all-gather.2.cloned.1.call-start = ((), (), s32[]{:S(2)}) async-start(), calls=%async_computation.4 | async-start | bytes 13369344 | tf_op jit(solution)/shard_map/all_gather | solution.py:83
  30.7 204.6 %reduce-scatter.3.cloned.1.call-start = ((), (), s32[]{:S(2)}) async-start(), calls=%async_computation.5 | async-start | bytes 13369344 | tf_op jit(solution)/shard_map/reduce_scatter | solution.py:90
  140.8 111.9 %copy-start.1 = (bf16[128,2048]{1,0:T(8,128)(2,1)S(1)}, bf16[128,2048]{1,0:T(8,128)(2,1)}, u32[]{:S(2)}) copy-start(bf16[128,2048]{1,0:T(8,128)(2,1)} %param.13) | copy-start | bytes 1572868
  140.8 112.3 %copy-start.2 = (f32[8,2048]{1,0:T(8,128)S(1)}, f32[8,2048]{1,0:T(8,128)}, u32[]{:S(2)}) copy-start(f32[8,2048]{1,0:T(8,128)} %param.20) | copy-start | bytes 196612
  235.3 17.4 %all-to-all-start.1 = ((bf16[8,24,2048]{2,1,0:T(8,128)(2,1)}), bf16[8,24,2048]{2,1,0:T(8,128)(2,1)S(1)}, u32[]{:S(2)}, u32[]{:S(2)}) async-start(bf16[8,24,2048]{2,1,0:T(8,128)(2,1)} %bitcast.23), calls=%async_computation.2 | async-start | bytes 1572864 | tf_op jit(solution)/shard_map/all_to_all | solution.py:96
  239.6 108.3 %reduce-scatter.5.cloned.1.call-start = ((), (), s32[]{:S(2)}) async-start(), calls=%async_computation.6 | async-start | bytes 4718592 | tf_op jit(solution)/shard_map/reduce_scatter | solution.py:115
  253.1 3.9 %copy-start.3 = (f32[2048]{0:T(1024)S(1)}, f32[2048]{0:T(1024)}, u32[]{:S(2)}) copy-start(f32[2048]{0:T(1024)} %param.21) | copy-start | bytes 24580
  258.1 40.7 %copy-start.5 = (f32[1024]{0:T(1024)S(1)}, f32[1024]{0:T(1024)}, u32[]{:S(2)}) copy-start(f32[1024]{0:T(1024)} %param.23) | copy-start | bytes 12292
  258.1 9.9 %collective-permute-start = (bf16[128,2048]{1,0:T(8,128)(2,1)S(1)}, bf16[128,2048]{1,0:T(8,128)(2,1)}, u32[]{:S(2)}, u32[]{:S(2)}) collective-permute-start(bf16[128,2048]{1,0:T(8,128)(2,1)S(1)} %get-tuple-element.6), channel_id=1, source_target_pairs={{0,16},{16,32},{32,48},{48,64},{64,80},{80,96},{96,112},{112,0},{1... | collective-permute-start | bytes 1572872 | tf_op jit(solution)/shard_map/ppermute | solution.py:16
  258.1 9.9 %collective-permute-start.1 = (bf16[128,2048]{1,0:T(8,128)(2,1)S(1)}, bf16[128,2048]{1,0:T(8,128)(2,1)}, u32[]{:S(2)}, u32[]{:S(2)}) collective-permute-start(bf16[128,2048]{1,0:T(8,128)(2,1)S(1)} %get-tuple-element.6), channel_id=1, source_target_pairs={{0,112},{16,0},{32,16},{48,32},{64,48},{80,64},{96,80},{112,96},{1... | collective-permute-start | bytes 1572872 | tf_op jit(solution)/shard_map/ppermute | solution.py:21
  268.0 10.1 %collective-permute-start.2 = (bf16[128,2048]{1,0:T(8,128)(2,1)}, bf16[128,2048]{1,0:T(8,128)(2,1)}, u32[]{:S(2)}, u32[]{:S(2)}) collective-permute-start(bf16[128,2048]{1,0:T(8,128)(2,1)} %collective-permute-done), channel_id=1, source_target_pairs={{0,16},{16,32},{32,48},{48,64},{64,80},{80,96},{96,112},{112,0},{1... | collective-permute-start | bytes 1572872 | tf_op jit(solution)/shard_map/ppermute | solution.py:16
  268.0 13.9 %collective-permute-start.3 = (bf16[128,2048]{1,0:T(8,128)(2,1)}, bf16[128,2048]{1,0:T(8,128)(2,1)}, u32[]{:S(2)}, u32[]{:S(2)}) collective-permute-start(bf16[128,2048]{1,0:T(8,128)(2,1)} %collective-permute-done.1), channel_id=1, source_target_pairs={{0,112},{16,0},{32,16},{48,32},{64,48},{80,64},{96,80},{112,96},{1... | collective-permute-start | bytes 1572872 | tf_op jit(solution)/shard_map/ppermute | solution.py:21
  278.1 10.0 %collective-permute-start.4 = (bf16[128,2048]{1,0:T(8,128)(2,1)}, bf16[128,2048]{1,0:T(8,128)(2,1)S(1)}, u32[]{:S(2)}, u32[]{:S(2)}) collective-permute-start(bf16[128,2048]{1,0:T(8,128)(2,1)} %collective-permute-done.2), channel_id=1, source_target_pairs={{0,16},{16,32},{32,48},{48,64},{64,80},{80,96},{96,112},{112,0},{1... | collective-permute-start | bytes 1572872 | tf_op jit(solution)/shard_map/ppermute | solution.py:16
  281.9 9.9 %collective-permute-start.5 = (bf16[128,2048]{1,0:T(8,128)(2,1)}, bf16[128,2048]{1,0:T(8,128)(2,1)S(1)}, u32[]{:S(2)}, u32[]{:S(2)}) collective-permute-start(bf16[128,2048]{1,0:T(8,128)(2,1)} %collective-permute-done.3), channel_id=1, source_target_pairs={{0,112},{16,0},{32,16},{48,32},{64,48},{80,64},{96,80},{112,96},{1... | collective-permute-start | bytes 1572872 | tf_op jit(solution)/shard_map/ppermute | solution.py:21
  288.2 9.8 %collective-permute-start.6 = (bf16[128,2048]{1,0:T(8,128)(2,1)S(1)}, bf16[128,2048]{1,0:T(8,128)(2,1)S(1)}, u32[]{:S(2)}, u32[]{:S(2)}) collective-permute-start(bf16[128,2048]{1,0:T(8,128)(2,1)S(1)} %collective-permute-done.4), channel_id=1, source_target_pairs={{0,16},{16,32},{32,48},{48,64},{64,80},{80,96},{96,112},{112,0},{1... | collective-permute-start | bytes 1572872 | tf_op jit(solution)/shard_map/ppermute | solution.py:16
  313.2 34.7 %copy-start.4 = (f32[2048]{0:T(1024)S(1)}, f32[2048]{0:T(1024)}, u32[]{:S(2)}) copy-start(f32[2048]{0:T(1024)} %param.25) | copy-start | bytes 24580
Sparse Core Ops, SparseCore 0:
  30.8 90.4 all-gather.1
  141.0 94.2 reduce-scatter.2
  313.3 34.5 reduce-scatter.4
